TPU v7x, 256 devices: a whole 4x4x8 slice. The times are simulated.
256 devices in a mesh: roll: 4 (over z_lo, core), mach: 16 (over y, x), cross: 4 (over z_hi).
Axes of the slice: x: 4, y: 4, z: 8 (z_hi: 4, z_lo: 2; z = z_hi * 2 + z_lo), core: 2. Of those that a mesh axis runs over, the one named last changes fastest.
Arguments:
- density: bfloat16 [128, 4096, 2048], P('roll', 'mach', 'cross'), may hold values from 0 to 1
- roll_start: float32 [32, 128], P(None, 'roll'), may hold values from 0.05 to 1
- mach_factor: bfloat16 [32, 4096], P(None, 'mach'), may hold values from 0.0099487305 to 1
- cross_factor: bfloat16 [32, 2048], P(None, 'cross'), may hold values from 0.0099487305 to 1
Outputs:
- roll_factor: float32 [32, 128], P(None, 'roll')
- mode_two: float32 [32, 4096], P(None, ('mach', 'cross'))
All inputs are finite; a program needn't handle non-finite values.
Results may differ from a plain program's by a relative error of at most 0.0003.
Values sent between devices are 32-bit elements; how exact they have to be, the bound alone decides.
A program may use at most 64 MiB of HBM per device.

v0:
```python
import jax
import jax.numpy as jnp
from jax import lax
from jax.sharding import PartitionSpec as P


def hals_rows(roll_rows, mttkrp, gram):

    def column_step(column, rows):
        column = jnp.asarray(column).astype(jnp.int32)
        gram_row = lax.dynamic_slice_in_dim(gram, column, 1, 0)
        diag_entry = lax.dynamic_slice_in_dim(gram_row, column, 1, 1)
        current = lax.dynamic_slice_in_dim(rows, column, 1, 0)
        target = lax.dynamic_slice_in_dim(mttkrp, column, 1, 0)
        mixed = jnp.dot(gram_row, rows, precision=lax.Precision.HIGHEST)
        updated = jnp.maximum(current + (target - mixed) / diag_entry, 0.0)
        return lax.dynamic_update_slice_in_dim(rows, updated, column, 0)

    return lax.fori_loop(0, roll_rows.shape[0], column_step, roll_rows)


def local(density, roll_start, mach_factor, cross_factor):
    rolls_here, bins_here, cross_here = density.shape
    rank = cross_factor.shape[0]
    flat = density.reshape(rolls_here * bins_here, cross_here)
    partial_value = lax.dot_general(
        cross_factor, flat, (((1,), (1,)), ((), ())), preferred_element_type=jnp.float32
    )
    partial_value = partial_value.reshape(rank, rolls_here, bins_here)
    local_terms = jnp.einsum(
        "rij,rj->ri",
        partial_value,
        mach_factor.astype(jnp.float32),
        precision=lax.Precision.HIGHEST,
    )
    local_mach = jnp.dot(mach_factor, mach_factor.T, preferred_element_type=jnp.float32)
    local_cross = jnp.dot(cross_factor, cross_factor.T, preferred_element_type=jnp.float32)
    mttkrp = lax.psum(local_terms, ("mach", "cross"))
    gram_mach = lax.psum(local_mach, "mach")
    gram_cross = lax.psum(local_cross, "cross")
    gram = gram_mach * gram_cross
    roll_factor = hals_rows(roll_start, mttkrp, gram)
    term = jnp.einsum("rij,ri->rj", partial_value, roll_factor, precision=lax.Precision.HIGHEST)
    whole = lax.psum(term, ("roll", "cross"))
    span = whole.shape[1] // lax.axis_size("cross")
    total = lax.dynamic_slice_in_dim(whole, lax.axis_index("cross") * span, span, 1)
    all_rolls = rolls_here * lax.axis_size("roll")
    all_cross = cross_here * lax.axis_size("cross")
    scale = rank / (all_rolls * all_cross)
    mode_two = total * scale
    return (roll_factor, mode_two)


def solution(mesh):
    in_specs = (P("roll", "mach", "cross"), P(None, "roll"), P(None, "mach"), P(None, "cross"))
    out_specs = (P(None, "roll"), P(None, ("mach", "cross")))
    return jax.shard_map(local, mesh=mesh, in_specs=in_specs, out_specs=out_specs, check_vma=False)
```

profile of v0, /device:TPU:1, one launch (start us, length us, event | category | flops | bytes accessed | tf_op | source)
XLA Modules:
  0.0 584.9 jit_solution(14968535453906031717)
XLA Ops:
  0.7 0.7 copy-done
  1.4 5.9 %fusion.9 = f32[32,32,256]{2,0,1:T(8,128)S(1)} fusion(bf16[32,256,512]{2,1,0:T(8,128)(2,1)} %param.6, bf16[32,512]{1,0:T(8,128)(2,1)S(1)} %copy-done), kind=kOutput, calls=%fused_computation.12 | convolution fusion | flops 268435456 | bytes 9469952 | tf_op jit(solution)/shard_map/dot_general | solution.py:26
  7.3 1.2 fusion.7
  8.5 327.1 %psum.28 = f32[32,32]{1,0:T(8,128)S(1)} all-reduce(f32[32,32]{1,0:T(8,128)S(1)} %bitcast.34), channel_id=1, replica_groups=mesh['roll'=4,'mach'=16,'cross'=4] {'mach','cross'}, use_global_device_ids=true, to_apply=%region_2.0 | all-reduce | flops 1024 | bytes 8192 | tf_op jit(solution)/shard_map/psum | solution.py:38
  335.7 56.2 %psum.29 = f32[32,32]{1,0:T(8,128)S(1)} all-reduce(f32[32,32]{1,0:T(8,128)S(1)} %fusion.12), channel_id=1, replica_groups=mesh['roll'=4,'mach'=16,'cross'=4] {'mach'}, use_global_device_ids=true, to_apply=%region_0.0 | all-reduce | flops 1024 | bytes 8192 | tf_op jit(solution)/shard_map/psum | solution.py:39
  392.0 12.7 %psum.30 = f32[32,32]{1,0:T(8,128)S(1)} all-reduce(f32[32,32]{1,0:T(8,128)S(1)} %fusion.13), channel_id=1, replica_groups=mesh['roll'=4,'mach'=16,'cross'=4] {'cross'}, use_global_device_ids=true, to_apply=%region_1.0 | all-reduce | flops 1024 | bytes 8192 | tf_op jit(solution)/shard_map/psum | solution.py:40
  404.7 45.2 %while.16 = (s32[]{:T(128)}, f32[32,32]{1,0:T(8,128)S(1)}, f32[32,32]{1,0:T(8,128)S(1)}, f32[32,32]{1,0:T(8,128)S(1)}, s32[]{:T(128)}, /*index=5*/s32[]{:T(128)}, s32[]{:T(128)}) while((s32[]{:T(128)}, f32[32,32]{1,0:T(8,128)S(1)}, f32[32,32]{1,0:T(8,128)S(1)}, f32[32,32]{1,0:T(8,128)S(1)}, s32[]{:T(128)}, /*index=5*/s32[]{:T(128)}, ...), condition=%wide.region_4.0_spmd, body=%wide.region_3.0_spmd.sunk | while | flops 12419 | bytes 19449 | solution.py:19
  404.7 0.6 dynamic_slice.66
  405.3 0.8 fusion.26
  406.1 0.6 dynamic_slice.66
  406.7 0.8 fusion.26
  407.6 0.6 dynamic_slice.66
  408.1 0.8 fusion.26
  409.0 0.6 dynamic_slice.66
  409.6 0.8 fusion.26
  411.0 0.8 fusion.26
  412.4 0.8 fusion.26
  413.8 0.8 fusion.26
  415.2 0.8 fusion.26
  416.6 0.8 fusion.26
  418.0 0.8 fusion.26
  418.8 0.6 dynamic_slice.66
  419.4 0.8 fusion.26
  420.8 0.8 fusion.26
  422.3 0.8 fusion.26
  423.7 0.8 fusion.26
  425.1 0.8 fusion.26
  426.5 0.8 fusion.26
  427.9 0.8 fusion.26
  429.3 0.8 fusion.26
  430.7 0.8 fusion.26
  432.1 0.8 fusion.26
  433.6 0.8 fusion.26
  435.0 0.8 fusion.26
  436.4 0.8 fusion.26
  437.8 0.8 fusion.26
  439.2 0.8 fusion.26
  440.6 0.8 fusion.26
  442.0 0.8 fusion.26
  443.4 0.8 fusion.26
  444.8 0.8 fusion.26
  445.7 0.6 dynamic_slice.66
  446.3 0.8 fusion.26
  447.7 0.8 fusion.26
  449.1 0.8 fusion.26
  449.9 1.3 fusion.5
  451.2 133.1 %psum.31 = f32[32,256]{1,0:T(8,128)S(1)} all-reduce(f32[32,256]{1,0:T(8,128)S(1)} %bitcast.33), channel_id=1, replica_groups=mesh['roll'=4,'mach'=16,'cross'=4] {'roll','cross'}, use_global_device_ids=true, to_apply=%region_5.0 | all-reduce | flops 8192 | bytes 65536 | tf_op jit(solution)/shard_map/psum | solution.py:44
  584.3 0.7 dynamic-slice_multiply_fusion
  (69 shorter events, 16.4 us)
Async XLA Ops:
  0.6 0.8 copy-start
  0.6 404.1 %copy-start.2 = (f32[32,32]{1,0:T(8,128)S(1)}, f32[32,32]{1,0:T(8,128)}, u32[]{:S(2)}) copy-start(f32[32,32]{1,0:T(8,128)} %param.7) | copy-start | bytes 12292
  0.7 6.6 %copy-start.3 = (bf16[32,256]{1,0:T(8,128)(2,1)S(1)}, bf16[32,256]{1,0:T(8,128)(2,1)}, u32[]{:S(2)}) copy-start(bf16[32,256]{1,0:T(8,128)(2,1)} %param.8) | copy-start | bytes 49156
  449.9 135.0 %copy-start.1 = (f32[32,32]{1,0:T(8,128)}, f32[32,32]{1,0:T(8,128)S(1)}, u32[]{:S(2)}) copy-start(f32[32,32]{1,0:T(8,128)S(1)} %get-tuple-element.124) | copy-start | bytes 12292
where the time goes:
time: 585 us
  blocking collectives  529 us (90%)
  matrix products  33.6 us (6%)
  local copies, waits for them, and re-layouts  20.4 us (3%)
    psum x1, blocking collectives, local(): mttkrp = lax.psum(local_terms, ('mach', 'cross'))  327 us
    psum x1, blocking collectives, local(): whole = lax.psum(term, ('roll', 'cross'))  133 us
    psum x1, blocking collectives, local(): gram_mach = lax.psum(local_mach, 'mach')  56.2 us
    dot_general x32, matrix products, column_step(): mixed = jnp.dot(gram_row, rows, precision=lax.Precision.HIGHEST)  25 us
    dynamic_slice x32, local copies, waits for them, and re-layouts, column_step(): diag_entry = lax.dynamic_slice_in_dim(gram_row, column, 1, 1)  18.8 us
    psum x1, blocking collectives, local(): gram_cross = lax.psum(local_cross, 'cross')  12.7 us

commit v1 on v0

--- a/solution.py
+++ b/solution.py
@@ -35,7 +35,8 @@
     )
     local_mach = jnp.dot(mach_factor, mach_factor.T, preferred_element_type=jnp.float32)
     local_cross = jnp.dot(cross_factor, cross_factor.T, preferred_element_type=jnp.float32)
-    mttkrp = lax.psum(local_terms, ("mach", "cross"))
+    inner = lax.psum(local_terms, "cross")
+    mttkrp = lax.psum(inner, "mach")
     gram_mach = lax.psum(local_mach, "mach")
     gram_cross = lax.psum(local_cross, "cross")
     gram = gram_mach * gram_cross

time: 585 us -> 214 us (0.37)
  blocking collectives: 529 us -> 158 us
    psum x3 -> x2, blocking collectives: 396 us -> 80.3 us  [the longest x1 60.8 us: local(): mttkrp = lax.psum(inner, 'mach')]
    psum x1, blocking collectives: 133 us -> 77.6 us  [local(): whole = lax.psum(term, ('roll', 'cross'))]
where the time goes in v1:
time: 214 us
  blocking collectives  158 us (74%)
  matrix products  33.6 us (16%)
  local copies, waits for them, and re-layouts  20.4 us (10%)
    psum x1, blocking collectives, local(): whole = lax.psum(term, ('roll', 'cross'))  77.6 us
    psum x1, blocking collectives, local(): mttkrp = lax.psum(inner, 'mach')  60.8 us
    dot_general x32, matrix products, column_step(): mixed = jnp.dot(gram_row, rows, precision=lax.Precision.HIGHEST)  25 us
    psum x1, blocking collectives, local(): inner = lax.psum(local_terms, 'cross')  19.5 us
    dynamic_slice x32, local copies, waits for them, and re-layouts, column_step(): diag_entry = lax.dynamic_slice_in_dim(gram_row, column, 1, 1)  18.8 us
    dot_general x1, matrix products, local(): lax.dot_general(cross_factor, flat, (((1,), (1,)), ((), ())), preferred_e...  5.9 us

profile of v1, /device:TPU:1, one launch (start us, length us, event | category | flops | bytes accessed | tf_op | source)
XLA Modules:
  0.0 213.8 jit_solution(8567797768996771899)
XLA Ops:
  0.7 0.7 copy-done
  1.4 5.9 %fusion.9 = f32[32,32,256]{2,0,1:T(8,128)S(1)} fusion(bf16[32,256,512]{2,1,0:T(8,128)(2,1)} %param.6, bf16[32,512]{1,0:T(8,128)(2,1)S(1)} %copy-done), kind=kOutput, calls=%fused_computation.12 | convolution fusion | flops 268435456 | bytes 9469952 | tf_op jit(solution)/shard_map/dot_general | solution.py:26
  7.3 1.2 fusion.7
  8.6 19.5 %all-reduce.1 = (f32[32,32]{1,0:T(8,128)S(1)}, f32[32,32]{1,0:T(8,128)S(1)}) all-reduce(f32[32,32]{1,0:T(8,128)S(1)} %bitcast.34, f32[32,32]{1,0:T(8,128)S(1)} %fusion.13), channel_id=1, replica_groups=mesh['roll'=4,'mach'=16,'cross'=4] {'cross'}, use_global_device_ids=true, to_apply=%region_2.0 | all-reduce | flops 2048 | bytes 16384 | tf_op jit(solution)/shard_map/psum | solution.py:38
  28.2 60.8 %all-reduce = (f32[32,32]{1,0:T(8,128)S(1)}, f32[32,32]{1,0:T(8,128)S(1)}) all-reduce(f32[32,32]{1,0:T(8,128)S(1)} %get-tuple-element.137, f32[32,32]{1,0:T(8,128)S(1)} %fusion.12), channel_id=1, replica_groups=mesh['roll'=4,'mach'=16,'cross'=4] {'mach'}, use_global_device_ids=true, to_apply=%region_3.0 | all-reduce | flops 2048 | bytes 16384 | tf_op jit(solution)/shard_map/psum | solution.py:39
  89.0 45.2 %while.16 = (s32[]{:T(128)}, f32[32,32]{1,0:T(8,128)S(1)}, f32[32,32]{1,0:T(8,128)S(1)}, f32[32,32]{1,0:T(8,128)S(1)}, s32[]{:T(128)}, /*index=5*/s32[]{:T(128)}, s32[]{:T(128)}) while((s32[]{:T(128)}, f32[32,32]{1,0:T(8,128)S(1)}, f32[32,32]{1,0:T(8,128)S(1)}, f32[32,32]{1,0:T(8,128)S(1)}, s32[]{:T(128)}, /*index=5*/s32[]{:T(128)}, ...), condition=%wide.region_5.0_spmd, body=%wide.region_4.0_spmd.sunk | while | flops 12419 | bytes 19949 | solution.py:19
  89.0 0.6 dynamic_slice.66
  89.6 0.8 fusion.26
  90.4 0.6 dynamic_slice.66
  91.0 0.8 fusion.26
  91.8 0.6 dynamic_slice.66
  92.4 0.8 fusion.26
  93.3 0.6 dynamic_slice.66
  93.8 0.8 fusion.26
  94.7 0.6 dynamic_slice.66
  95.3 0.8 fusion.26
  96.1 0.6 dynamic_slice.66
  96.7 0.8 fusion.26
  98.1 0.8 fusion.26
  99.5 0.8 fusion.26
  100.9 0.8 fusion.26
  102.3 0.8 fusion.26
  103.7 0.8 fusion.26
  105.1 0.8 fusion.26
  106.5 0.8 fusion.26
  108.0 0.8 fusion.26
  109.4 0.8 fusion.26
  110.8 0.8 fusion.26
  112.2 0.8 fusion.26
  113.6 0.8 fusion.26
  115.0 0.8 fusion.26
  116.4 0.8 fusion.26
  117.8 0.8 fusion.26
  119.3 0.8 fusion.26
  120.7 0.8 fusion.26
  122.1 0.8 fusion.26
  122.9 0.6 dynamic_slice.66
  123.5 0.8 fusion.26
  124.9 0.8 fusion.26
  126.3 0.8 fusion.26
  127.7 0.8 fusion.26
  129.1 0.8 fusion.26
  130.5 0.8 fusion.26
  132.0 0.8 fusion.26
  133.4 0.8 fusion.26
  134.2 1.3 fusion.5
  135.5 77.6 %psum.39 = f32[32,256]{1,0:T(8,128)S(1)} all-reduce(f32[32,256]{1,0:T(8,128)S(1)} %bitcast.33), channel_id=1, replica_groups=mesh['roll'=4,'mach'=16,'cross'=4] {'roll','cross'}, use_global_device_ids=true, to_apply=%region_6.0 | all-reduce | flops 8192 | bytes 65536 | tf_op jit(solution)/shard_map/psum | solution.py:45
  213.1 0.7 dynamic-slice_multiply_fusion
  (68 shorter events, 15.8 us)
Async XLA Ops:
  0.6 0.8 copy-start
  0.6 6.7 %copy-start.3 = (bf16[32,256]{1,0:T(8,128)(2,1)S(1)}, bf16[32,256]{1,0:T(8,128)(2,1)}, u32[]{:S(2)}) copy-start(bf16[32,256]{1,0:T(8,128)(2,1)} %param.8) | copy-start | bytes 49156
  0.7 88.3 %copy-start.2 = (f32[32,32]{1,0:T(8,128)S(1)}, f32[32,32]{1,0:T(8,128)}, u32[]{:S(2)}) copy-start(f32[32,32]{1,0:T(8,128)} %param.7) | copy-start | bytes 12292
  134.2 79.6 %copy-start.1 = (f32[32,32]{1,0:T(8,128)}, f32[32,32]{1,0:T(8,128)S(1)}, u32[]{:S(2)}) copy-start(f32[32,32]{1,0:T(8,128)S(1)} %get-tuple-element.124) | copy-start | bytes 12292

commit v2 on v0

--- a/solution.py
+++ b/solution.py
@@ -41,7 +41,9 @@
     gram = gram_mach * gram_cross
     roll_factor = hals_rows(roll_start, mttkrp, gram)
     term = jnp.einsum("rij,ri->rj", partial_value, roll_factor, precision=lax.Precision.HIGHEST)
-    whole = lax.psum(term, ("roll", "cross"))
+    whole = term
+    for name in ("roll", "cross"):
+        whole = lax.psum(whole, name)
     span = whole.shape[1] // lax.axis_size("cross")
     total = lax.dynamic_slice_in_dim(whole, lax.axis_index("cross") * span, span, 1)
     all_rolls = rolls_here * lax.axis_size("roll")

time: 585 us -> 552 us (0.944)
  blocking collectives: 529 us -> 493 us
    psum x1 -> x2, blocking collectives: 133 us -> 96.9 us  [local(): whole = lax.psum(whole, name)]
where the time goes in v2:
time: 552 us; the launch traced here: 549 us
  blocking collectives  493 us (89%)
  matrix products  33.6 us (6%)
  local copies, waits for them, and re-layouts  20.4 us (4%)
    psum x1, blocking collectives, local(): mttkrp = lax.psum(local_terms, ('mach', 'cross'))  327 us
    psum x2, blocking collectives, local(): whole = lax.psum(whole, name)  96.9 us
    psum x1, blocking collectives, local(): gram_mach = lax.psum(local_mach, 'mach')  56.2 us
    dot_general x32, matrix products, column_step(): mixed = jnp.dot(gram_row, rows, precision=lax.Precision.HIGHEST)  25 us
    dynamic_slice x32, local copies, waits for them, and re-layouts, column_step(): diag_entry = lax.dynamic_slice_in_dim(gram_row, column, 1, 1)  18.8 us
    psum x1, blocking collectives, local(): gram_cross = lax.psum(local_cross, 'cross')  12.7 us

profile of v2, /device:TPU:1, one launch (start us, length us, event | category | flops | bytes accessed | tf_op | source)
XLA Modules:
  0.0 548.8 jit_solution(7887763289000505743)
XLA Ops:
  0.7 0.7 copy-done
  1.4 5.9 %fusion.9 = f32[32,32,256]{2,0,1:T(8,128)S(1)} fusion(bf16[32,256,512]{2,1,0:T(8,128)(2,1)} %param.6, bf16[32,512]{1,0:T(8,128)(2,1)S(1)} %copy-done), kind=kOutput, calls=%fused_computation.12 | convolution fusion | flops 268435456 | bytes 9469952 | tf_op jit(solution)/shard_map/dot_general | solution.py:26
  7.3 1.2 fusion.7
  8.5 327.1 %psum.35 = f32[32,32]{1,0:T(8,128)S(1)} all-reduce(f32[32,32]{1,0:T(8,128)S(1)} %bitcast.34), channel_id=1, replica_groups=mesh['roll'=4,'mach'=16,'cross'=4] {'mach','cross'}, use_global_device_ids=true, to_apply=%region_2.0 | all-reduce | flops 1024 | bytes 8192 | tf_op jit(solution)/shard_map/psum | solution.py:38
  335.7 56.2 %psum.36 = f32[32,32]{1,0:T(8,128)S(1)} all-reduce(f32[32,32]{1,0:T(8,128)S(1)} %fusion.12), channel_id=1, replica_groups=mesh['roll'=4,'mach'=16,'cross'=4] {'mach'}, use_global_device_ids=true, to_apply=%region_0.0 | all-reduce | flops 1024 | bytes 8192 | tf_op jit(solution)/shard_map/psum | solution.py:39
  392.0 12.7 %psum.37 = f32[32,32]{1,0:T(8,128)S(1)} all-reduce(f32[32,32]{1,0:T(8,128)S(1)} %fusion.13), channel_id=1, replica_groups=mesh['roll'=4,'mach'=16,'cross'=4] {'cross'}, use_global_device_ids=true, to_apply=%region_1.0 | all-reduce | flops 1024 | bytes 8192 | tf_op jit(solution)/shard_map/psum | solution.py:40
  404.7 45.2 %while.16 = (s32[]{:T(128)}, f32[32,32]{1,0:T(8,128)S(1)}, f32[32,32]{1,0:T(8,128)S(1)}, f32[32,32]{1,0:T(8,128)S(1)}, s32[]{:T(128)}, /*index=5*/s32[]{:T(128)}, s32[]{:T(128)}) while((s32[]{:T(128)}, f32[32,32]{1,0:T(8,128)S(1)}, f32[32,32]{1,0:T(8,128)S(1)}, f32[32,32]{1,0:T(8,128)S(1)}, s32[]{:T(128)}, /*index=5*/s32[]{:T(128)}, ...), condition=%wide.region_4.0_spmd, body=%wide.region_3.0_spmd.sunk | while | flops 12419 | bytes 19449 | solution.py:19
  404.7 0.6 dynamic_slice.66
  405.3 0.8 fusion.26
  406.1 0.6 dynamic_slice.66
  406.7 0.8 fusion.26
  407.6 0.6 dynamic_slice.66
  408.1 0.8 fusion.26
  409.6 0.8 fusion.26
  411.0 0.8 fusion.26
  412.4 0.8 fusion.26
  413.8 0.8 fusion.26
  415.2 0.8 fusion.26
  416.6 0.8 fusion.26
  418.0 0.8 fusion.26
  418.8 0.6 dynamic_slice.66
  419.4 0.8 fusion.26
  420.8 0.8 fusion.26
  422.3 0.8 fusion.26
  423.7 0.8 fusion.26
  425.1 0.8 fusion.26
  426.5 0.8 fusion.26
  427.9 0.8 fusion.26
  429.3 0.8 fusion.26
  430.7 0.8 fusion.26
  432.1 0.8 fusion.26
  433.6 0.8 fusion.26
  435.0 0.8 fusion.26
  436.4 0.8 fusion.26
  437.8 0.8 fusion.26
  439.2 0.8 fusion.26
  440.6 0.8 fusion.26
  442.0 0.8 fusion.26
  443.4 0.8 fusion.26
  444.8 0.8 fusion.26
  445.7 0.6 dynamic_slice.66
  446.3 0.8 fusion.26
  447.7 0.8 fusion.26
  449.1 0.8 fusion.26
  449.9 1.3 fusion.5
  451.2 81.9 %psum.38 = f32[32,256]{1,0:T(8,128)S(1)} all-reduce(f32[32,256]{1,0:T(8,128)S(1)} %bitcast.33), channel_id=1, replica_groups=mesh['roll'=4,'mach'=16,'cross'=4] {'roll'}, use_global_device_ids=true, to_apply=%region_5.0 | all-reduce | flops 8192 | bytes 65536 | tf_op jit(solution)/shard_map/psum | solution.py:46
  533.0 15.1 %psum.39 = f32[32,256]{1,0:T(8,128)S(1)} all-reduce(f32[32,256]{1,0:T(8,128)S(1)} %psum.38), channel_id=1, replica_groups=mesh['roll'=4,'mach'=16,'cross'=4] {'cross'}, use_global_device_ids=true, to_apply=%region_6.0 | all-reduce | flops 8192 | bytes 65536 | tf_op jit(solution)/shard_map/psum | solution.py:46
  548.1 0.7 dynamic-slice_multiply_fusion
  (70 shorter events, 17.0 us)
Async XLA Ops:
  0.6 0.8 copy-start
  0.6 404.1 %copy-start.2 = (f32[32,32]{1,0:T(8,128)S(1)}, f32[32,32]{1,0:T(8,128)}, u32[]{:S(2)}) copy-start(f32[32,32]{1,0:T(8,128)} %param.7) | copy-start | bytes 12292
  0.7 6.6 %copy-start.3 = (bf16[32,256]{1,0:T(8,128)(2,1)S(1)}, bf16[32,256]{1,0:T(8,128)(2,1)}, u32[]{:S(2)}) copy-start(bf16[32,256]{1,0:T(8,128)(2,1)} %param.8) | copy-start | bytes 49156
  449.9 98.9 %copy-start.1 = (f32[32,32]{1,0:T(8,128)}, f32[32,32]{1,0:T(8,128)S(1)}, u32[]{:S(2)}) copy-start(f32[32,32]{1,0:T(8,128)S(1)} %get-tuple-element.124) | copy-start | bytes 12292

commit v3 on v0

--- a/solution.py
+++ b/solution.py
@@ -20,6 +20,10 @@
 
 
 def local(density, roll_start, mach_factor, cross_factor):
+
+    def teams_take(message):
+        return jnp.sum(lax.all_gather(message, axis_name=("roll", "cross")), 0)
+
     rolls_here, bins_here, cross_here = density.shape
     rank = cross_factor.shape[0]
     flat = density.reshape(rolls_here * bins_here, cross_here)
@@ -41,7 +45,7 @@
     gram = gram_mach * gram_cross
     roll_factor = hals_rows(roll_start, mttkrp, gram)
     term = jnp.einsum("rij,ri->rj", partial_value, roll_factor, precision=lax.Precision.HIGHEST)
-    whole = lax.psum(term, ("roll", "cross"))
+    whole = teams_take(term)
     span = whole.shape[1] // lax.axis_size("cross")
     total = lax.dynamic_slice_in_dim(whole, lax.axis_index("cross") * span, span, 1)
     all_rolls = rolls_here * lax.axis_size("roll")

time: 585 us -> 558 us (0.954)
  blocking collectives: 529 us -> 502 us
    psum x1 -> x0, blocking collectives: 133 us -> none  [local(): whole = lax.psum(term, ('roll', 'cross'))]
    all_gather x0 -> x1, blocking collectives: none -> 106 us  [teams_take(): return jnp.sum(lax.all_gather(message, axis_name=('roll', 'cross')), 0)]
where the time goes in v3:
time: 558 us
  blocking collectives  502 us (90%)
  matrix products  33.6 us (6%)
  local copies, waits for them, and re-layouts  20.4 us (4%)
    psum x1, blocking collectives, local(): mttkrp = lax.psum(local_terms, ('mach', 'cross'))  327 us
    all_gather x1, blocking collectives, teams_take(): return jnp.sum(lax.all_gather(message, axis_name=('roll', 'cross')), 0)  106 us
    psum x1, blocking collectives, local(): gram_mach = lax.psum(local_mach, 'mach')  56.2 us
    dot_general x32, matrix products, column_step(): mixed = jnp.dot(gram_row, rows, precision=lax.Precision.HIGHEST)  25 us
    dynamic_slice x32, local copies, waits for them, and re-layouts, column_step(): diag_entry = lax.dynamic_slice_in_dim(gram_row, column, 1, 1)  18.8 us
    psum x1, blocking collectives, local(): gram_cross = lax.psum(local_cross, 'cross')  12.7 us

profile of v3, /device:TPU:1, one launch (start us, length us, event | category | flops | bytes accessed | tf_op | source)
XLA Modules:
  0.0 557.8 jit_solution(10372697452723228785)
XLA Ops:
  0.7 0.7 copy-done
  1.4 5.9 %fusion.9 = f32[32,32,256]{2,0,1:T(8,128)S(1)} fusion(bf16[32,256,512]{2,1,0:T(8,128)(2,1)} %param.6, bf16[32,512]{1,0:T(8,128)(2,1)S(1)} %copy-done), kind=kOutput, calls=%fused_computation.12 | convolution fusion | flops 268435456 | bytes 9469952 | tf_op jit(solution)/shard_map/dot_general | solution.py:30
  7.3 1.2 fusion.7
  8.5 327.1 %psum.21 = f32[32,32]{1,0:T(8,128)S(1)} all-reduce(f32[32,32]{1,0:T(8,128)S(1)} %bitcast.36), channel_id=1, replica_groups=mesh['roll'=4,'mach'=16,'cross'=4] {'mach','cross'}, use_global_device_ids=true, to_apply=%region_2.0 | all-reduce | flops 1024 | bytes 8192 | tf_op jit(solution)/shard_map/psum | solution.py:42
  335.7 56.2 %psum.22 = f32[32,32]{1,0:T(8,128)S(1)} all-reduce(f32[32,32]{1,0:T(8,128)S(1)} %fusion.12), channel_id=1, replica_groups=mesh['roll'=4,'mach'=16,'cross'=4] {'mach'}, use_global_device_ids=true, to_apply=%region_0.0 | all-reduce | flops 1024 | bytes 8192 | tf_op jit(solution)/shard_map/psum | solution.py:43
  392.0 12.7 %psum.23 = f32[32,32]{1,0:T(8,128)S(1)} all-reduce(f32[32,32]{1,0:T(8,128)S(1)} %fusion.13), channel_id=1, replica_groups=mesh['roll'=4,'mach'=16,'cross'=4] {'cross'}, use_global_device_ids=true, to_apply=%region_1.0 | all-reduce | flops 1024 | bytes 8192 | tf_op jit(solution)/shard_map/psum | solution.py:44
  404.7 45.2 %while.16 = (s32[]{:T(128)}, f32[32,32]{1,0:T(8,128)S(1)}, f32[32,32]{1,0:T(8,128)S(1)}, f32[32,32]{1,0:T(8,128)S(1)}, s32[]{:T(128)}, /*index=5*/s32[]{:T(128)}, s32[]{:T(128)}) while((s32[]{:T(128)}, f32[32,32]{1,0:T(8,128)S(1)}, f32[32,32]{1,0:T(8,128)S(1)}, f32[32,32]{1,0:T(8,128)S(1)}, s32[]{:T(128)}, /*index=5*/s32[]{:T(128)}, ...), condition=%wide.region_4.0_spmd, body=%wide.region_3.0_spmd.sunk | while | flops 12419 | bytes 19449 | solution.py:19
  404.7 0.6 dynamic_slice.66
  405.3 0.8 fusion.26
  406.1 0.6 dynamic_slice.66
  406.7 0.8 fusion.26
  407.6 0.6 dynamic_slice.66
  408.1 0.8 fusion.26
  409.0 0.6 dynamic_slice.66
  409.6 0.8 fusion.26
  411.0 0.8 fusion.26
  412.4 0.8 fusion.26
  413.8 0.8 fusion.26
  415.2 0.8 fusion.26
  416.6 0.8 fusion.26
  418.0 0.8 fusion.26
  418.8 0.6 dynamic_slice.66
  419.4 0.8 fusion.26
  420.8 0.8 fusion.26
  422.3 0.8 fusion.26
  423.7 0.8 fusion.26
  425.1 0.8 fusion.26
  426.5 0.8 fusion.26
  427.9 0.8 fusion.26
  429.3 0.8 fusion.26
  430.7 0.8 fusion.26
  432.1 0.8 fusion.26
  433.6 0.8 fusion.26
  435.0 0.8 fusion.26
  436.4 0.8 fusion.26
  437.8 0.8 fusion.26
  439.2 0.8 fusion.26
  440.6 0.8 fusion.26
  442.0 0.8 fusion.26
  443.4 0.8 fusion.26
  444.8 0.8 fusion.26
  445.7 0.6 dynamic_slice.66
  446.3 0.8 fusion.26
  447.7 0.8 fusion.26
  449.1 0.8 fusion.26
  449.9 1.3 fusion.5
  451.2 105.9 %all-gather = f32[512,256]{1,0:T(8,128)S(1)} all-gather(f32[32,256]{1,0:T(8,128)S(1)} %bitcast.35), channel_id=2, replica_groups=mesh['roll'=4,'mach'=16,'cross'=4] {'roll','cross'}, dimensions={0}, use_global_device_ids=true | all-gather | bytes 557056 | tf_op jit(solution)/shard_map/all_gather | solution.py:25
  557.1 0.7 dynamic-slice_multiply_fusion
  (70 shorter events, 16.4 us)
Async XLA Ops:
  0.6 0.8 copy-start
  0.6 404.1 %copy-start.2 = (f32[32,32]{1,0:T(8,128)S(1)}, f32[32,32]{1,0:T(8,128)}, u32[]{:S(2)}) copy-start(f32[32,32]{1,0:T(8,128)} %param.7) | copy-start | bytes 12292
  0.7 6.6 %copy-start.3 = (bf16[32,256]{1,0:T(8,128)(2,1)S(1)}, bf16[32,256]{1,0:T(8,128)(2,1)}, u32[]{:S(2)}) copy-start(bf16[32,256]{1,0:T(8,128)(2,1)} %param.8) | copy-start | bytes 49156
  449.9 107.9 %copy-start.1 = (f32[32,32]{1,0:T(8,128)}, f32[32,32]{1,0:T(8,128)S(1)}, u32[]{:S(2)}) copy-start(f32[32,32]{1,0:T(8,128)S(1)} %get-tuple-element.124) | copy-start | bytes 12292
